TPU v7x, 32 devices: a whole 2x2x4 slice. The times are simulated.
32 devices in a mesh: group: 2 (over y), ctx: 4 (over z), head: 4 (over x, core).
Axes of the slice: x: 2, y: 2, z: 4, core: 2. Of those that a mesh axis runs over, the one named last changes fastest.
Arguments:
- query: bfloat16 [1024, 4096], P(('group', 'ctx'), 'head'), parts along dimension 0, may hold values from -8 to 8
- keys: bfloat16 [1024, 512], P(('group', 'ctx'), 'head'), parts along dimension 0, may hold values from -6 to 6
- values: bfloat16 [1024, 512], P(('group', 'ctx'), 'head'), parts along dimension 0, may hold values from -6 to 6
- residual: bfloat16 [1024, 2048], P(('group', 'ctx', 'head')), parts along dimension 0, may hold values from -15 to 15
- o_weight: bfloat16 [4096, 2048], P('head', 'ctx'), may hold values from -0.09375 to 0.09375
- gain: float32 [2048], replicated, may hold values from 0.1 to 1.9
- routes: int32 [1024, 8], P(('group', 'ctx', 'head')), parts along dimension 0, may hold values from 0 to 15, all different within a row; in each aligned block of 32 rows (0 to 31, 32 to 63, ...) at most 32 rows name the same one
- gates: float32 [1024, 8], P(('group', 'ctx', 'head')), parts along dimension 0, may hold values from 0.05 to 1
- w_gate: bfloat16 [16, 2048, 768], P(('ctx', 'head')), may hold values from -0.125 to 0.125
- w_up: bfloat16 [16, 2048, 768], P(('ctx', 'head')), may hold values from -0.125 to 0.125
- w_down: bfloat16 [16, 768, 2048], P(('ctx', 'head')), may hold values from -0.625 to 0.625
Outputs:
- mixed: bfloat16 [1024, 2048], P(('group', 'ctx', 'head')), parts along dimension 0
- expert_mix: bfloat16 [1024, 2048], P(('group', 'ctx', 'head')), parts along dimension 0
There are 2 independent parts, one for each index of `group`. A program takes and returns all parts, laid end to end along the dimension named above; an argument that names none is the same for every part. Nothing has to cross between parts.
Inputs may be any that keep to these rules, and one draw needn't show every extreme that they name: `routes`: the 8 experts of a token are distinct. In each aligned block of 32 tokens (the tokens of one owner device), no expert is named more than 32 times, a bound that some block reaches.
All inputs are finite; a program needn't handle non-finite values.
Results may differ from a plain program's by a relative error of at most 0.019.
Values may be sent and summed in bfloat16 or wider, within the bound.
No kernel may reach another device: no remote copies, remote signals or barrier semaphores. Data moves between devices by JAX's collectives and lax.ppermute only.
A program may use at most 128 MiB of HBM per device.

v0:
```python
import jax
import jax.numpy as jnp
from jax import lax
from jax.sharding import PartitionSpec as P

HEAD_DIMENSION = 128


def expert_apply(arrived, gate_proj, up_proj, down_proj):
    shape_in = arrived.shape
    flat_rows = arrived.reshape(-1, shape_in[-1])
    gate_act = jnp.dot(flat_rows, gate_proj, preferred_element_type=jnp.float32)
    up_act = jnp.dot(flat_rows, up_proj, preferred_element_type=jnp.float32)
    hidden = (jax.nn.silu(gate_act) * up_act).astype(jnp.bfloat16)
    output = jnp.dot(hidden, down_proj, preferred_element_type=jnp.float32).astype(jnp.bfloat16)
    return output.reshape(shape_in)


def body(query, keys, values, residual, o_weight, gain, routes, gates, w_gate, w_up, w_down):
    head_size = HEAD_DIMENSION
    query_rows = query.shape[0]
    kv_heads = keys.shape[1] // head_size
    q_heads = query.shape[1] // head_size
    head_replicas = q_heads // kv_heads
    scale = head_size ** (-0.5)
    queries = query.reshape(query_rows, kv_heads, head_replicas, head_size)
    first_pos = lax.axis_index("ctx") * query_rows
    query_pos = first_pos + jnp.arange(query_rows, dtype=jnp.int32)
    last_pos = first_pos + query_rows - 1

    def accumulate(carry, pieces):
        run_max, run_sum, run_acc = carry
        key_piece, value_piece = pieces
        width = key_piece.shape[0]
        key_pos = jnp.arange(width, dtype=jnp.int32)
        visible = key_pos[None, :] <= query_pos[:, None]
        scores = (
            jnp.einsum(
                "veqi,zei->eqvz",
                queries,
                key_piece.reshape(width, kv_heads, head_size),
                preferred_element_type=jnp.float32,
            )
            * scale
        )
        scores = jnp.where(visible, scores, -1e30)
        new_max = jnp.maximum(run_max, jnp.max(scores, axis=-1))
        weights = jnp.where(visible, jnp.exp(scores - new_max[..., None]), 0.0)
        new_sum = jnp.sum(weights, axis=-1)
        update = jnp.einsum(
            "pexa,apo->pexo",
            weights.astype(jnp.bfloat16),
            value_piece.reshape(width, kv_heads, head_size),
            preferred_element_type=jnp.float32,
        )
        return (new_max, new_sum, update)

    start_state = (
        jnp.full((kv_heads, head_replicas, query_rows), -1e30, jnp.float32),
        jnp.zeros((kv_heads, head_replicas, query_rows), jnp.float32),
        jnp.zeros((kv_heads, head_replicas, query_rows, head_size), jnp.float32),
    )
    pieces = (
        lax.all_gather(keys, "ctx", axis=0, tiled=True),
        lax.all_gather(values, "ctx", axis=0, tiled=True),
    )
    run_max, run_sum, run_acc = lax.cond(
        jnp.int32(0) > last_pos, lambda: start_state, lambda: accumulate(start_state, pieces)
    )
    attended = (
        (run_acc / run_sum[..., None])
        .transpose(2, 0, 1, 3)
        .reshape(query_rows, q_heads * head_size)
        .astype(jnp.bfloat16)
    )
    head_terms = jnp.dot(
        attended,
        lax.all_gather(o_weight, "ctx", axis=1, tiled=True),
        preferred_element_type=jnp.float32,
    )
    summed = lax.psum_scatter(
        head_terms.astype(jnp.bfloat16), "head", scatter_dimension=0, tiled=True
    ).astype(jnp.float32)
    mixed = (summed + residual.astype(jnp.float32)).astype(jnp.bfloat16)
    mixed_f = mixed.astype(jnp.float32)
    normed = (
        mixed_f * lax.rsqrt(jnp.mean(mixed_f * mixed_f, axis=-1, keepdims=True) + 1e-06) * gain
    ).astype(jnp.bfloat16)
    own_rows = residual.shape[0]
    model_dim = residual.shape[1]
    top_count = routes.shape[1]
    ctx_count = lax.axis_size("ctx")
    head_count = lax.axis_size("head")
    devices = ctx_count * head_count
    capacity = min(own_rows, max(2, 2 * own_rows * top_count // devices))
    expert_ids = routes.reshape(-1)
    onehot = (expert_ids[:, None] == jnp.arange(devices, dtype=jnp.int32)[None, :]).astype(
        jnp.int32
    )
    slots = jnp.sum((jnp.cumsum(onehot, axis=0) - 1) * onehot, axis=1)
    target = expert_ids * capacity + slots
    outgoing = (
        jnp.zeros((devices * capacity, model_dim), jnp.bfloat16)
        .at[target]
        .set(jnp.repeat(normed, top_count, axis=0))
    )
    outgoing = outgoing.reshape(devices, capacity, model_dim)
    gate_proj = w_gate[0]
    up_proj = w_up[0]
    down_proj = w_down[0]
    computed = expert_apply(
        lax.all_to_all(outgoing, ("ctx", "head"), split_axis=0, concat_axis=0, tiled=True),
        gate_proj,
        up_proj,
        down_proj,
    )
    returned = lax.all_to_all(computed, ("ctx", "head"), split_axis=0, concat_axis=0, tiled=True)
    selected_entries = returned.reshape(devices * capacity, model_dim)[target]
    selected_entries = selected_entries.astype(jnp.float32).reshape(own_rows, top_count, model_dim)
    weight_norm = gates / jnp.sum(gates, axis=-1, keepdims=True)
    expert_mix = jnp.sum(selected_entries * weight_norm[..., None], axis=1).astype(jnp.bfloat16)
    return (mixed, expert_mix)


def solution(mesh):
    return jax.shard_map(
        body,
        mesh=mesh,
        in_specs=(
            P(("group", "ctx"), "head"),
            P(("group", "ctx"), "head"),
            P(("group", "ctx"), "head"),
            P(("group", "ctx", "head"), None),
            P("head", "ctx"),
            P(),
            P(("group", "ctx", "head"), None),
            P(("group", "ctx", "head"), None),
            P(("ctx", "head"), None, None),
            P(("ctx", "head"), None, None),
            P(("ctx", "head"), None, None),
        ),
        out_specs=(P(("group", "ctx", "head"), None), P(("group", "ctx", "head"), None)),
        check_vma=False,
    )
```

profile of v0, /device:TPU:11, one launch (start us, length us, event | category | flops | bytes accessed | tf_op | source)
XLA Modules:
  0.0 255.7 jit_solution(5889170970731669494)
XLA Ops:
  7.2 0.7 all-gather.2.cloned.1.call-update
  8.0 11.0 %all_gather.10 = bf16[512,128]{1,0:T(8,128)(2,1)S(1)} all-gather(bf16[128,128]{1,0:T(8,128)(2,1)} %param.15), channel_id=1, replica_groups=mesh['group'=2,'ctx'=4,'head'=4] {'ctx'}, dimensions={0}, use_global_device_ids=true | all-gather | bytes 163840 | tf_op jit(solution)/shard_map/all_gather | solution.py:65
  19.0 14.5 %all_gather.9 = bf16[512,128]{1,0:T(8,128)(2,1)S(1)} all-gather(bf16[128,128]{1,0:T(8,128)(2,1)} %param.14), channel_id=1, replica_groups=mesh['group'=2,'ctx'=4,'head'=4] {'ctx'}, dimensions={0}, use_global_device_ids=true | all-gather | bytes 163840 | tf_op jit(solution)/shard_map/all_gather | solution.py:64
  33.5 2.6 %conditional.1 = (f32[1,8,128]{2,1,0:T(8,128)S(1)}, f32[1,8,128,128]{2,3,1,0:T(8,128)S(1)}) conditional(s32[]{:T(128)} %convert_element_type.54, (s32[]{:T(128)}, s32[128]{0:T(128)S(1)}, bf16[128,1024]{1,0:T(8,128)(2,1)}, bf16[512,128]{1,0:T(8,128)(2,1)S(1)}, bf16[512,128]{1,0:T(8,128)(2,1)S(1)}) %tuple.16, () %tuple.17), branch_computations={%region_0.3_spmd, %region_3.4_spmd} | conditional | flops 275315840 | bytes 7628308 | solution.py:67
  33.5 0.1 iota_compare_fusion
  33.6 1.4 fusion
  35.0 0.6 convolution_bitcast_fusion
  35.6 0.5 fusion.2
  36.2 0.1 divide_convert_fusion
  36.2 55.0 %all-gather.2.cloned.1.call-done = bf16[1024,2048]{1,0:T(8,128)(2,1)} async-done(((bf16[1024,512]{1,0:T(8,128)(2,1)}), bf16[1024,2048]{1,0:T(8,128)(2,1)}) %all-gather.2.cloned.1.call-update) | async-done | bytes 4194320 | tf_op jit(solution)/shard_map/all_gather | solution.py:78
  91.2 3.8 %convolution_convert_fusion = bf16[128,2048]{1,0:T(8,128)(2,1)} fusion(bf16[128,1024]{0,1:T(8,128)(2,1)S(1)} %bitcast.93, bf16[1024,2048]{1,0:T(8,128)(2,1)} %all-gather.2.cloned.1.call-done), kind=kOutput, calls=%fused_computation.32 | convolution fusion | flops 537133056 | bytes 4980736 | tf_op jit(solution)/shard_map/dot_general | solution.py:76
  95.0 0.1 copy.21
  95.1 0.1 eq.29
  95.2 0.1 eq.25
  95.3 0.6 reduce-window.6
  95.9 0.2 slice_reduce_fusion
  96.1 0.1 copy.20
  96.2 0.1 mul.68
  96.3 0.1 fusion.40
  96.4 20.1 %reduce-scatter.2.cloned.1.call-done = bf16[32,2048]{1,0:T(8,128)(2,1)} async-done(((bf16[128,2048]{1,0:T(8,128)(2,1)}), bf16[32,2048]{1,0:T(8,128)(2,1)}) %reduce-scatter.2.cloned.1.call-update) | async-done | bytes 131088 | tf_op jit(solution)/shard_map/reduce_scatter | solution.py:81
  116.5 1.1 fusion.36
  117.6 0.1 fusion.38
  117.7 3.7 %scatter_custom_fusion = bf16[512,2048]{1,0:T(8,128)(2,1)} fusion(s32[256]{0:T(256)S(1)} %bitcast.96, bf16[]{:T(256)} %constant.28.clone.1, bf16[32,2048]{1,0:T(8,128)(2,1)S(1)} %fusion.38), kind=kCustom, calls=%fused_computation.36 | custom fusion | bytes 2228226 | tf_op jit(solution)/shard_map/scatter | solution.py:105
  121.5 54.1 %all_to_all.10 = bf16[16,32,2048]{2,1,0:T(8,128)(2,1)S(1)} all-to-all(bf16[16,32,2048]{2,1,0:T(8,128)(2,1)} %bitcast.89), channel_id=1, replica_groups=mesh['group'=2,'ctx'=4,'head'=4] {'ctx','head'}, dimensions={0} | all-to-all | bytes 4194304 | tf_op jit(solution)/shard_map/all_to_all | solution.py:112
  175.5 1.3 copy-done.1
  176.8 3.0 %fusion.22 = f32[512,768]{1,0:T(8,128)} fusion(bf16[512,2048]{1,0:T(8,128)(2,1)S(1)} %bitcast.91, bf16[1,2048,768]{2,1,0:T(8,128)(2,1)S(1)} %copy-done.7), kind=kOutput, calls=%fused_computation.29 | convolution fusion | flops 1610612736 | bytes 6815744 | tf_op jit(solution)/shard_map/dot_general | solution.py:12
  179.8 8.3 %fusion.24 = bf16[512,2048]{1,0:T(8,128)(2,1)} fusion(bf16[1,768,2048]{2,1,0:T(8,128)(2,1)S(1)} %copy-done, f32[512,768]{1,0:T(8,128)} %fusion.22, bf16[512,2048]{1,0:T(8,128)(2,1)} %bitcast.92, bf16[1,2048,768]{2,1,0:T(8,128)(2,1)} %param.22), kind=kOutput, calls=%fused_computation.31 | convolution fusion | flops 3224633344 | bytes 12058624 | tf_op jit(solution)/shard_map/dot_general | solution.py:15
  188.1 5.2 %all-to-all-start.1 = ((bf16[16,32,2048]{2,1,0:T(8,128)(2,1)}), bf16[16,32,2048]{2,1,0:T(8,128)(2,1)}, u32[]{:S(2)}, u32[]{:S(2)}) async-start(bf16[16,32,2048]{2,1,0:T(8,128)(2,1)} %bitcast.90), calls=%async_computation.2 | async-start | bytes 4194304 | tf_op jit(solution)/shard_map/all_to_all | solution.py:117
  193.3 0.1 copy.24
  193.4 47.4 %all-to-all-done.1 = bf16[16,32,2048]{2,1,0:T(8,128)(2,1)} async-done(((bf16[16,32,2048]{2,1,0:T(8,128)(2,1)}), bf16[16,32,2048]{2,1,0:T(8,128)(2,1)}, u32[]{:S(2)}, u32[]{:S(2)}) %all-to-all-start.1) | async-done | bytes 2097184 | tf_op jit(solution)/shard_map/all_to_all | solution.py:117
  240.8 5.2 %gather_fusion = bf16[256,2048]{1,0:T(8,128)(2,1)} fusion(bf16[512,2048]{1,0:T(8,128)(2,1)} %bitcast.20, s32[1024]{0:T(1024)S(1)} %pad_clamp_fusion), kind=kCustom, calls=%fused_computation | custom fusion | bytes 2098176 | tf_op jit(solution)/shard_map/gather | solution.py:118
  246.0 2.9 %fusion.27 = bf16[32,2048]{1,0:T(8,128)(2,1)} fusion(bf16[256,2048]{1,0:T(8,128)(2,1)} %gather_fusion, f32[32,8]{1,0:T(8,128)S(1)} %copy.24), kind=kLoop, calls=%fused_computation.34 | loop fusion | flops 1507328 | bytes 1180672 | tf_op jit(solution)/shard_map/reduce_sum | solution.py:121
  (30 shorter events, 0.2 us)
Async XLA Ops:
  7.2 172.6 %copy-start = (bf16[1,768,2048]{2,1,0:T(8,128)(2,1)S(1)}, bf16[1,768,2048]{2,1,0:T(8,128)(2,1)}, u32[]{:S(2)}) copy-start(bf16[1,768,2048]{2,1,0:T(8,128)(2,1)} %param.23) | copy-start | bytes 9437188
  7.2 84.0 %all-gather.2.cloned.1.call-start = ((), (), s32[]{:S(2)}) async-start(), calls=%async_computation.3 | async-start | bytes 5242880 | tf_op jit(solution)/shard_map/all_gather | solution.py:78
  7.9 108.6 %reduce-scatter.2.cloned.1.call-start = ((), (), s32[]{:S(2)}) async-start(), calls=%async_computation.4 | async-start | bytes 655360 | tf_op jit(solution)/shard_map/reduce_scatter | solution.py:81
  91.2 3.8 %copy-start.4 = (s32[32,8]{0,1:T(8,128)S(1)}, s32[32,8]{0,1:T(8,128)}, u32[]{:S(2)}) copy-start(s32[32,8]{0,1:T(8,128)} %param.19) | copy-start | bytes 3076
  91.2 25.3 %copy-start.3 = (bf16[32,2048]{1,0:T(8,128)(2,1)S(1)}, bf16[32,2048]{1,0:T(8,128)(2,1)}, u32[]{:S(2)}) copy-start(bf16[32,2048]{1,0:T(8,128)(2,1)} %param.16) | copy-start | bytes 393220
  91.2 26.4 %copy-start.6 = (f32[2048]{0:T(1024)S(1)}, f32[2048]{0:T(1024)}, u32[]{:S(2)}) copy-start(f32[2048]{0:T(1024)} %param.18) | copy-start | bytes 24580
  117.6 58.0 %copy-start.2 = (bf16[32,2048]{1,0:T(8,128)(2,1)}, bf16[32,2048]{1,0:T(8,128)(2,1)S(1)}, u32[]{:S(2)}) copy-start(bf16[32,2048]{1,0:T(8,128)(2,1)S(1)} %get-tuple-element.28) | copy-start | bytes 393220
  121.5 55.4 %copy-start.7 = (bf16[1,2048,768]{2,1,0:T(8,128)(2,1)S(1)}, bf16[1,2048,768]{2,1,0:T(8,128)(2,1)}, u32[]{:S(2)}) copy-start(bf16[1,2048,768]{2,1,0:T(8,128)(2,1)} %param.21) | copy-start | bytes 9437188
  175.5 1.3 copy-start.1
  188.1 5.2 %copy-start.5 = (f32[32,8]{0,1:T(8,128)S(1)}, f32[32,8]{0,1:T(8,128)}, u32[]{:S(2)}) copy-start(f32[32,8]{0,1:T(8,128)} %param.20) | copy-start | bytes 3076
  188.1 52.7 %all-to-all-start.1 = ((bf16[16,32,2048]{2,1,0:T(8,128)(2,1)}), bf16[16,32,2048]{2,1,0:T(8,128)(2,1)}, u32[]{:S(2)}, u32[]{:S(2)}) async-start(bf16[16,32,2048]{2,1,0:T(8,128)(2,1)} %bitcast.90), calls=%async_computation.2 | async-start | bytes 4194304 | tf_op jit(solution)/shard_map/all_to_all | solution.py:117
Sparse Core Ops, SparseCore 0:
  9.6 81.6 all-gather.1
  95.1 21.3 reduce-scatter.1
where the time goes:
time: 256 us
  waiting for transfers between devices  123 us (48%)
  blocking collectives  79.6 us (31%)
  matrix products  17.1 us (7%)
  between operations  14.1 us (6%)
  local copies, waits for them, and re-layouts  11 us (4%)
  other arithmetic  5.41 us (2%)
  starting transfers between devices  5.23 us (2%)
    all_gather x1, waiting for transfers between devices, body(): lax.all_gather(o_weight, 'ctx', axis=1, tiled=True)  55 us
    all_to_all x1, blocking collectives, body(): lax.all_to_all(outgoing, ('ctx', 'head'), split_axis=0, concat_axis=0, ti...  54.1 us
    all_to_all x1, waiting for transfers between devices, body(): lax.all_to_all(computed, ('ctx', 'head'), split_axis=0, concat_axis=0, ti...  47.4 us
    reduce_scatter x1, waiting for transfers between devices, body(): lax.psum_scatter(head_terms.astype(jnp.bfloat16), 'head', scatter_dimensi...  20.1 us
    all_gather x1, blocking collectives, body(): lax.all_gather(keys, 'ctx', axis=0, tiled=True)  14.5 us
    all_gather x1, blocking collectives, body(): lax.all_gather(values, 'ctx', axis=0, tiled=True)  11 us
    dot_general x1, matrix products, expert_apply(): jnp.dot(hidden, down_proj, preferred_element_type=jnp.float32)  8.28 us
    gather x1, local copies, waits for them, and re-layouts, body(): selected_entries = returned.reshape(devices * capacity, model_dim)[target]  5.21 us
  transfers between devices with their start and end apart: 3, of which 3 were waited for; matrix products, arithmetic and copies ran while one was open for 2% of the time, Pallas kernels for 0%

commit v1 on v0

--- a/solution.py
+++ b/solution.py
@@ -4,6 +4,17 @@
 from jax.sharding import PartitionSpec as P
 
 HEAD_DIMENSION = 128
+
+
+def in_blocks(value, dim, size):
+    before, after = (value.shape[:dim], value.shape[dim + 1 :])
+    return jnp.moveaxis(value.reshape(*before, size, -1, *after), dim, 0)
+
+
+def joined_along(tiles, dim):
+    dims = list(tiles.shape[1:])
+    dims[dim] *= tiles.shape[0]
+    return jnp.moveaxis(tiles, 0, dim).reshape(dims)
 
 
 def expert_apply(arrived, gate_proj, up_proj, down_proj):
@@ -114,7 +125,17 @@
         up_proj,
         down_proj,
     )
-    returned = lax.all_to_all(computed, ("ctx", "head"), split_axis=0, concat_axis=0, tiled=True)
+    peers, here = (lax.axis_size(("ctx", "head")), lax.axis_index(("ctx", "head")))
+    pieces_2 = in_blocks(computed, 0, peers)
+    out = pieces_2
+    for turn in range(1, peers):
+        target_2, source = ((here + turn) % peers, (here - turn) % peers)
+        sent = lax.dynamic_index_in_dim(pieces_2, target_2, 0)
+        received = lax.ppermute(
+            sent, ("ctx", "head"), [(i, (i + turn) % peers) for i in range(peers)]
+        )
+        out = lax.dynamic_update_slice_in_dim(out, received, source, axis=0)
+    returned = joined_along(out, 0)
     selected_entries = returned.reshape(devices * capacity, model_dim)[target]
     selected_entries = selected_entries.astype(jnp.float32).reshape(own_rows, top_count, model_dim)
     weight_norm = gates / jnp.sum(gates, axis=-1, keepdims=True)

time: 256 us -> 269 us (1.051)
  blocking collectives: 79.6 us -> 25.5 us
  waiting for transfers between devices: 123 us -> 148 us
  starting transfers between devices: 5.23 us -> 27.8 us
  local copies, waits for them, and re-layouts: 11 us -> 24.2 us
    all_to_all x1 -> x0, blocking collectives: 54.1 us -> none  [body(): lax.all_to_all(outgoing, ('ctx', 'head'), split_axis=0, concat_axis=0, ti...]
    ppermute x0 -> x15, waiting for transfers between devices: none -> 24.3 us  [body(): lax.ppermute(sent, ('ctx', 'head'), [(i, (i + turn) % peers) for i in ran...]
    ppermute x0 -> x15, starting transfers between devices: none -> 21.2 us  [body(): lax.ppermute(sent, ('ctx', 'head'), [(i, (i + turn) % peers) for i in ran...]
    dynamic_update_slice x0 -> x14, local copies, waits for them, and re-layouts: none -> 10.1 us  [body(): out = lax.dynamic_update_slice_in_dim(out, received, source, axis=0)]
    dynamic_slice x0 -> x2, local copies, waits for them, and re-layouts: none -> 3.6 us  [body(): sent = lax.dynamic_index_in_dim(pieces_2, target_2, 0)]
  transfers between devices with their start and end apart: 3 -> 18, of which waited for: 3 -> 9; matrix products, arithmetic and copies ran while one was open for 2% -> 6% of each run, Pallas kernels for 0% -> 0%
where the time goes in v1:
time: 269 us; the launch traced here: 266 us
  waiting for transfers between devices  148 us (55%)
  starting transfers between devices  27.8 us (10%)
  blocking collectives  25.5 us (9%)
  local copies, waits for them, and re-layouts  24.2 us (9%)
  matrix products  19.6 us (7%)
  between operations  14.2 us (5%)
  other arithmetic  7.26 us (3%)
    all_gather x1, waiting for transfers between devices, body(): lax.all_gather(o_weight, 'ctx', axis=1, tiled=True)  55 us
    all_to_all x1, waiting for transfers between devices, body(): lax.all_to_all(outgoing, ('ctx', 'head'), split_axis=0, concat_axis=0, ti...  47.5 us
    ppermute x15, waiting for transfers between devices, body(): lax.ppermute(sent, ('ctx', 'head'), [(i, (i + turn) % peers) for i in ran...  24.3 us
    ppermute x15, starting transfers between devices, body(): lax.ppermute(sent, ('ctx', 'head'), [(i, (i + turn) % peers) for i in ran...  21.2 us
    reduce_scatter x1, waiting for transfers between devices, body(): lax.psum_scatter(head_terms.astype(jnp.bfloat16), 'head', scatter_dimensi...  20.1 us
    all_gather x1, blocking collectives, body(): lax.all_gather(keys, 'ctx', axis=0, tiled=True)  14.5 us
    all_gather x1, blocking collectives, body(): lax.all_gather(values, 'ctx', axis=0, tiled=True)  11 us
    dynamic_update_slice x14, local copies, waits for them, and re-layouts, body(): out = lax.dynamic_update_slice_in_dim(out, received, source, axis=0)  10.1 us
  transfers between devices with their start and end apart: 18, of which 9 were waited for; matrix products, arithmetic and copies ran while one was open for 6% of the time, Pallas kernels for 0%

profile of v1, /device:TPU:11, one launch (start us, length us, event | category | flops | bytes accessed | tf_op | source)
XLA Modules:
  0.0 266.2 jit_solution(3816744185799500039)
XLA Ops:
  8.0 11.0 %all_gather.10 = bf16[512,128]{1,0:T(8,128)(2,1)S(1)} all-gather(bf16[128,128]{1,0:T(8,128)(2,1)} %param.15), channel_id=1, replica_groups=mesh['group'=2,'ctx'=4,'head'=4] {'ctx'}, dimensions={0}, use_global_device_ids=true | all-gather | bytes 163840 | tf_op jit(solution)/shard_map/all_gather | solution.py:76
  19.0 14.5 %all_gather.9 = bf16[512,128]{1,0:T(8,128)(2,1)S(1)} all-gather(bf16[128,128]{1,0:T(8,128)(2,1)} %param.14), channel_id=1, replica_groups=mesh['group'=2,'ctx'=4,'head'=4] {'ctx'}, dimensions={0}, use_global_device_ids=true | all-gather | bytes 163840 | tf_op jit(solution)/shard_map/all_gather | solution.py:75
  33.5 2.6 conditional.1
  33.6 1.4 fusion
  36.2 55.0 %all-gather.2.cloned.1.call-done = bf16[1024,2048]{1,0:T(8,128)(2,1)} async-done(((bf16[1024,512]{1,0:T(8,128)(2,1)}), bf16[1024,2048]{1,0:T(8,128)(2,1)}) %all-gather.2.cloned.1.call-update) | async-done | bytes 4194320 | tf_op jit(solution)/shard_map/all_gather | solution.py:89
  91.2 3.8 %convolution_convert_fusion = bf16[128,2048]{1,0:T(8,128)(2,1)} fusion(bf16[128,1024]{0,1:T(8,128)(2,1)S(1)} %bitcast.93, bf16[1024,2048]{1,0:T(8,128)(2,1)} %all-gather.2.cloned.1.call-done), kind=kOutput, calls=%fused_computation.32 | convolution fusion | flops 537133056 | bytes 4980736 | tf_op jit(solution)/shard_map/dot_general | solution.py:87
  96.4 20.1 %reduce-scatter.2.cloned.1.call-done = bf16[32,2048]{1,0:T(8,128)(2,1)} async-done(((bf16[128,2048]{1,0:T(8,128)(2,1)}), bf16[32,2048]{1,0:T(8,128)(2,1)}) %reduce-scatter.2.cloned.1.call-update) | async-done | bytes 131088 | tf_op jit(solution)/shard_map/reduce_scatter | solution.py:92
  117.8 3.7 %scatter_custom_fusion = bf16[512,2048]{1,0:T(8,128)(2,1)} fusion(s32[256]{0:T(256)S(1)} %bitcast.96, bf16[]{:T(256)} %constant.230.clone.1, bf16[32,2048]{1,0:T(8,128)(2,1)S(1)} %fusion.38), kind=kCustom, calls=%fused_computation.36 | custom fusion | bytes 2228226 | tf_op jit(solution)/shard_map/scatter | solution.py:116
  121.5 6.5 %all-to-all-start = ((bf16[16,32,2048]{2,1,0:T(8,128)(2,1)}), bf16[16,32,2048]{2,1,0:T(8,128)(2,1)}, u32[]{:S(2)}, u32[]{:S(2)}) async-start(bf16[16,32,2048]{2,1,0:T(8,128)(2,1)} %bitcast.92), calls=%async_computation.1 | async-start | bytes 4194304 | tf_op jit(solution)/shard_map/all_to_all | solution.py:123
  128.0 47.5 %all-to-all-done = bf16[16,32,2048]{2,1,0:T(8,128)(2,1)} async-done(((bf16[16,32,2048]{2,1,0:T(8,128)(2,1)}), bf16[16,32,2048]{2,1,0:T(8,128)(2,1)}, u32[]{:S(2)}, u32[]{:S(2)}) %all-to-all-start) | async-done | bytes 2097184 | tf_op jit(solution)/shard_map/all_to_all | solution.py:123
  175.5 5.5 %fusion.22 = f32[512,768]{1,0:T(8,128)} fusion(bf16[512,2048]{1,0:T(8,128)(2,1)} %bitcast.15, bf16[1,2048,768]{2,1,0:T(8,128)(2,1)} %param.21), kind=kOutput, calls=%fused_computation.29 | convolution fusion | flops 1610612736 | bytes 6815744 | tf_op jit(solution)/shard_map/dot_general | solution.py:23
  181.0 8.3 %fusion.24 = bf16[512,2048]{1,0:T(8,128)(2,1)} fusion(bf16[1,768,2048]{2,1,0:T(8,128)(2,1)S(1)} %copy-done, f32[512,768]{1,0:T(8,128)} %fusion.22, bf16[512,2048]{1,0:T(8,128)(2,1)} %bitcast.15, bf16[1,2048,768]{2,1,0:T(8,128)(2,1)} %param.22), kind=kOutput, calls=%fused_computation.31 | convolution fusion | flops 3224633344 | bytes 12058624 | tf_op jit(solution)/shard_map/dot_general | solution.py:26
  190.2 1.7 collective-permute-start
  191.9 1.9 collective-permute-done
  193.9 2.7 %constant_dynamic-slice_fusion = (bf16[1,1,32,2048]{3,2,0,1:T(8,128)(2,1)S(1)}, bf16[1,1,32,2048]{3,2,0,1:T(8,128)(2,1)S(1)}, bf16[1,1,32,2048]{3,2,0,1:T(8,128)...) fusion(bf16[16,1,32,2048]{3,2,0,1:T(8,128)(2,1)} %bitcast.90, ...), kind=kLoop, calls=%fused_computation.56 | loop fusion | bytes 3932220 | tf_op jit(solution)/shard_map/jit(dynamic_index_in_dim)/dynamic_slice | solution.py:133
  197.9 1.3 pad_clamp_fusion
  199.2 1.1 collective-permute-start.2
  200.3 4.2 %collective-permute-start.3 = (bf16[1,1,32,2048]{3,2,0,1:T(8,128)(2,1)}, bf16[1,1,32,2048]{3,2,0,1:T(8,128)(2,1)S(1)}, u32[]{:S(2)}, u32[]{:S(2)}) collective-permute-start(bf16[1,1,32,2048]{3,2,0,1:T(8,128)(2,1)} %get-tuple-element.42), channel_id=1, source_target_pairs={{0,4},{1,5},{2,6},{3,7},{4,8},{5,9},{6,10},{7,11},{8,12},{9,13},{1... | collective-permute-start | bytes 393224 | tf_op jit(solution)/shard_map/ppermute | solution.py:134
  204.5 3.2 %collective-permute-start.5 = (bf16[1,1,32,2048]{3,2,0,1:T(8,128)(2,1)}, bf16[1,1,32,2048]{3,2,0,1:T(8,128)(2,1)S(1)}, u32[]{:S(2)}, u32[]{:S(2)}) collective-permute-start(bf16[1,1,32,2048]{3,2,0,1:T(8,128)(2,1)} %get-tuple-element.40), channel_id=1, source_target_pairs={{0,6},{1,7},{2,8},{3,9},{4,10},{5,11},{6,12},{7,13},{8,14},{9,15},... | collective-permute-start | bytes 393224 | tf_op jit(solution)/shard_map/ppermute | solution.py:134
  207.7 1.6 constant_dynamic-update-slice_fusion.13
  209.2 1.5 collective-permute-start.7
  211.4 1.8 collective-permute-start.8
  213.9 1.7 collective-permute-start.9
  216.2 13.0 %collective-permute-done.5 = bf16[1,1,32,2048]{3,2,0,1:T(8,128)(2,1)S(1)} collective-permute-done((bf16[1,1,32,2048]{3,2,0,1:T(8,128)(2,1)}, bf16[1,1,32,2048]{3,2,0,1:T(8,128)(2,1)S(1)}, u32[]{:S(2)}, u32[]{:S(2)}) %collective-permute-start.5) | collective-permute-done | bytes 131104 | tf_op jit(solution)/shard_map/ppermute | solution.py:134
  229.2 3.5 %collective-permute-start.10 = (bf16[1,1,32,2048]{3,2,0,1:T(8,128)(2,1)}, bf16[1,1,32,2048]{3,2,0,1:T(8,128)(2,1)S(1)}, u32[]{:S(2)}, u32[]{:S(2)}) collective-permute-start(bf16[1,1,32,2048]{3,2,0,1:T(8,128)(2,1)} %get-tuple-element.35), channel_id=1, source_target_pairs={{0,11},{1,12},{2,13},{3,14},{4,15},{5,0},{6,1},{7,2},{8,3},{9,4},{... | collective-permute-start | bytes 393224 | tf_op jit(solution)/shard_map/ppermute | solution.py:134
  233.3 1.3 collective-permute-done.6
  235.3 3.7 %collective-permute-done.7 = bf16[1,1,32,2048]{3,2,0,1:T(8,128)(2,1)S(1)} collective-permute-done((bf16[1,1,32,2048]{3,2,0,1:T(8,128)(2,1)}, bf16[1,1,32,2048]{3,2,0,1:T(8,128)(2,1)S(1)}, u32[]{:S(2)}, u32[]{:S(2)}) %collective-permute-start.7) | collective-permute-done | bytes 131104 | tf_op jit(solution)/shard_map/ppermute | solution.py:134
  239.7 2.4 collective-permute-start.13
  244.1 1.4 collective-permute-done.11
  246.9 3.0 %collective-permute-done.13 = bf16[1,1,32,2048]{3,2,0,1:T(8,128)(2,1)S(1)} collective-permute-done((bf16[1,1,32,2048]{3,2,0,1:T(8,128)(2,1)S(1)}, bf16[1,1,32,2048]{3,2,0,1:T(8,128)(2,1)S(1)}, u32[]{:S(2)}, u32[]{:S(2)}) %collective-permute-start.13) | collective-permute-done | bytes 131104 | tf_op jit(solution)/shard_map/ppermute | solution.py:134
  251.1 5.4 %gather_fusion = bf16[256,2048]{1,0:T(8,128)(2,1)} fusion(bf16[512,2048]{1,0:T(8,128)(2,1)} %bitcast.91, s32[1024]{0:T(1024)} %pad_clamp_fusion), kind=kCustom, calls=%fused_computation | custom fusion | bytes 2098176 | tf_op jit(solution)/shard_map/gather | solution.py:139
  256.5 2.9 %fusion.27 = bf16[32,2048]{1,0:T(8,128)(2,1)} fusion(bf16[256,2048]{1,0:T(8,128)(2,1)} %gather_fusion, f32[32,8]{1,0:T(8,128)S(1)} %copy.24), kind=kLoop, calls=%fused_computation.34 | loop fusion | flops 1507328 | bytes 1180672 | tf_op jit(solution)/shard_map/reduce_sum | solution.py:142
  (73 shorter events, 15.5 us)
Async XLA Ops:
  7.2 173.8 %copy-start = (bf16[1,768,2048]{2,1,0:T(8,128)(2,1)S(1)}, bf16[1,768,2048]{2,1,0:T(8,128)(2,1)}, u32[]{:S(2)}) copy-start(bf16[1,768,2048]{2,1,0:T(8,128)(2,1)} %param.23) | copy-start | bytes 9437188
  7.2 84.0 %all-gather.2.cloned.1.call-start = ((), (), s32[]{:S(2)}) async-start(), calls=%async_computation.2 | async-start | bytes 5242880 | tf_op jit(solution)/shard_map/all_gather | solution.py:89
  7.9 108.6 %reduce-scatter.2.cloned.1.call-start = ((), (), s32[]{:S(2)}) async-start(), calls=%async_computation.3 | async-start | bytes 655360 | tf_op jit(solution)/shard_map/reduce_scatter | solution.py:92
  91.2 3.8 %copy-start.3 = (s32[32,8]{0,1:T(8,128)S(1)}, s32[32,8]{0,1:T(8,128)}, u32[]{:S(2)}) copy-start(s32[32,8]{0,1:T(8,128)} %param.19) | copy-start | bytes 3076
  91.2 25.3 %copy-start.2 = (bf16[32,2048]{1,0:T(8,128)(2,1)S(1)}, bf16[32,2048]{1,0:T(8,128)(2,1)}, u32[]{:S(2)}) copy-start(bf16[32,2048]{1,0:T(8,128)(2,1)} %param.16) | copy-start | bytes 393220
  91.2 26.4 %copy-start.5 = (f32[2048]{0:T(1024)S(1)}, f32[2048]{0:T(1024)}, u32[]{:S(2)}) copy-start(f32[2048]{0:T(1024)} %param.18) | copy-start | bytes 24580
  96.4 25.1 %copy-start.6 = (s32[256,1]{0,1:T(1,128)}, s32[256,1]{0,1:T(1,128)S(1)}, u32[]{:S(2)}) copy-start(s32[256,1]{0,1:T(1,128)S(1)} %compare_select_fusion) | copy-start | bytes 3076
  117.6 3.9 %copy-start.1 = (bf16[32,2048]{1,0:T(8,128)(2,1)}, bf16[32,2048]{1,0:T(8,128)(2,1)S(1)}, u32[]{:S(2)}) copy-start(bf16[32,2048]{1,0:T(8,128)(2,1)S(1)} %get-tuple-element.28) | copy-start | bytes 393220
  121.5 54.0 %all-to-all-start = ((bf16[16,32,2048]{2,1,0:T(8,128)(2,1)}), bf16[16,32,2048]{2,1,0:T(8,128)(2,1)}, u32[]{:S(2)}, u32[]{:S(2)}) async-start(bf16[16,32,2048]{2,1,0:T(8,128)(2,1)} %bitcast.92), calls=%async_computation.1 | async-start | bytes 4194304 | tf_op jit(solution)/shard_map/all_to_all | solution.py:123
  181.0 10.9 %copy-start.4 = (f32[32,8]{0,1:T(8,128)S(1)}, f32[32,8]{0,1:T(8,128)}, u32[]{:S(2)}) copy-start(f32[32,8]{0,1:T(8,128)} %param.20) | copy-start | bytes 3076
  190.2 3.7 %collective-permute-start = (bf16[1,1,32,2048]{3,2,0,1:T(8,128)(2,1)S(1)}, bf16[1,1,32,2048]{3,2,0,1:T(8,128)(2,1)}, u32[]{:S(2)}, u32[]{:S(2)}) collective-permute-start(bf16[1,1,32,2048]{3,2,0,1:T(8,128)(2,1)S(1)} %constant_dynamic-slice_fusion.14), channel_id=1, source_target_pairs={{0,1},{1,2},{2,3},{3,4},{4,5},{5,6},{6,7},{7,8},{8,9},{9,10},{10,1... | collective-permute-start | bytes 393224 | tf_op jit(solution)/shard_map/ppermute | solution.py:134
  196.5 11.1 %collective-permute-start.1 = (bf16[1,1,32,2048]{3,2,0,1:T(8,128)(2,1)}, bf16[1,1,32,2048]{3,2,0,1:T(8,128)(2,1)}, u32[]{:S(2)}, u32[]{:S(2)}) collective-permute-start(bf16[1,1,32,2048]{3,2,0,1:T(8,128)(2,1)} %get-tuple-element.44), channel_id=1, source_target_pairs={{0,2},{1,3},{2,4},{3,5},{4,6},{5,7},{6,8},{7,9},{8,10},{9,11},{10,... | collective-permute-start | bytes 393224 | tf_op jit(solution)/shard_map/ppermute | solution.py:134
  199.2 10.0 %collective-permute-start.2 = (bf16[1,1,32,2048]{3,2,0,1:T(8,128)(2,1)}, bf16[1,1,32,2048]{3,2,0,1:T(8,128)(2,1)S(1)}, u32[]{:S(2)}, u32[]{:S(2)}) collective-permute-start(bf16[1,1,32,2048]{3,2,0,1:T(8,128)(2,1)} %get-tuple-element.43), channel_id=1, source_target_pairs={{0,3},{1,4},{2,5},{3,6},{4,7},{5,8},{6,9},{7,10},{8,11},{9,12},{10... | collective-permute-start | bytes 393224 | tf_op jit(solution)/shard_map/ppermute | solution.py:134
  200.3 11.1 %collective-permute-start.3 = (bf16[1,1,32,2048]{3,2,0,1:T(8,128)(2,1)}, bf16[1,1,32,2048]{3,2,0,1:T(8,128)(2,1)S(1)}, u32[]{:S(2)}, u32[]{:S(2)}) collective-permute-start(bf16[1,1,32,2048]{3,2,0,1:T(8,128)(2,1)} %get-tuple-element.42), channel_id=1, source_target_pairs={{0,4},{1,5},{2,6},{3,7},{4,8},{5,9},{6,10},{7,11},{8,12},{9,13},{1... | collective-permute-start | bytes 393224 | tf_op jit(solution)/shard_map/ppermute | solution.py:134
  204.5 9.4 %collective-permute-start.4 = (bf16[1,1,32,2048]{3,2,0,1:T(8,128)(2,1)}, bf16[1,1,32,2048]{3,2,0,1:T(8,128)(2,1)S(1)}, u32[]{:S(2)}, u32[]{:S(2)}) collective-permute-start(bf16[1,1,32,2048]{3,2,0,1:T(8,128)(2,1)} %get-tuple-element.41), channel_id=1, source_target_pairs={{0,5},{1,6},{2,7},{3,8},{4,9},{5,10},{6,11},{7,12},{8,13},{9,14},{... | collective-permute-start | bytes 393224 | tf_op jit(solution)/shard_map/ppermute | solution.py:134
  204.5 24.7 %collective-permute-start.5 = (bf16[1,1,32,2048]{3,2,0,1:T(8,128)(2,1)}, bf16[1,1,32,2048]{3,2,0,1:T(8,128)(2,1)S(1)}, u32[]{:S(2)}, u32[]{:S(2)}) collective-permute-start(bf16[1,1,32,2048]{3,2,0,1:T(8,128)(2,1)} %get-tuple-element.40), channel_id=1, source_target_pairs={{0,6},{1,7},{2,8},{3,9},{4,10},{5,11},{6,12},{7,13},{8,14},{9,15},... | collective-permute-start | bytes 393224 | tf_op jit(solution)/shard_map/ppermute | solution.py:134
  207.7 27.0 %collective-permute-start.6 = (bf16[1,1,32,2048]{3,2,0,1:T(8,128)(2,1)}, bf16[1,1,32,2048]{3,2,0,1:T(8,128)(2,1)S(1)}, u32[]{:S(2)}, u32[]{:S(2)}) collective-permute-start(bf16[1,1,32,2048]{3,2,0,1:T(8,128)(2,1)} %get-tuple-element.39), channel_id=1, source_target_pairs={{0,7},{1,8},{2,9},{3,10},{4,11},{5,12},{6,13},{7,14},{8,15},{9,0},... | collective-permute-start | bytes 393224 | tf_op jit(solution)/shard_map/ppermute | solution.py:134
  209.2 29.8 %collective-permute-start.7 = (bf16[1,1,32,2048]{3,2,0,1:T(8,128)(2,1)}, bf16[1,1,32,2048]{3,2,0,1:T(8,128)(2,1)S(1)}, u32[]{:S(2)}, u32[]{:S(2)}) collective-permute-start(bf16[1,1,32,2048]{3,2,0,1:T(8,128)(2,1)} %get-tuple-element.38), channel_id=1, source_target_pairs={{0,8},{1,9},{2,10},{3,11},{4,12},{5,13},{6,14},{7,15},{8,0},{9,1},... | collective-permute-start | bytes 393224 | tf_op jit(solution)/shard_map/ppermute | solution.py:134
  211.4 28.3 %collective-permute-start.8 = (bf16[1,1,32,2048]{3,2,0,1:T(8,128)(2,1)}, bf16[1,1,32,2048]{3,2,0,1:T(8,128)(2,1)S(1)}, u32[]{:S(2)}, u32[]{:S(2)}) collective-permute-start(bf16[1,1,32,2048]{3,2,0,1:T(8,128)(2,1)} %get-tuple-element.37), channel_id=1, source_target_pairs={{0,9},{1,10},{2,11},{3,12},{4,13},{5,14},{6,15},{7,0},{8,1},{9,2},... | collective-permute-start | bytes 393224 | tf_op jit(solution)/shard_map/ppermute | solution.py:134
  213.9 28.9 %collective-permute-start.9 = (bf16[1,1,32,2048]{3,2,0,1:T(8,128)(2,1)}, bf16[1,1,32,2048]{3,2,0,1:T(8,128)(2,1)S(1)}, u32[]{:S(2)}, u32[]{:S(2)}) collective-permute-start(bf16[1,1,32,2048]{3,2,0,1:T(8,128)(2,1)} %get-tuple-element.36), channel_id=1, source_target_pairs={{0,10},{1,11},{2,12},{3,13},{4,14},{5,15},{6,0},{7,1},{8,2},{9,3},... | collective-permute-start | bytes 393224 | tf_op jit(solution)/shard_map/ppermute | solution.py:134
  229.2 14.3 %collective-permute-start.10 = (bf16[1,1,32,2048]{3,2,0,1:T(8,128)(2,1)}, bf16[1,1,32,2048]{3,2,0,1:T(8,128)(2,1)S(1)}, u32[]{:S(2)}, u32[]{:S(2)}) collective-permute-start(bf16[1,1,32,2048]{3,2,0,1:T(8,128)(2,1)} %get-tuple-element.35), channel_id=1, source_target_pairs={{0,11},{1,12},{2,13},{3,14},{4,15},{5,0},{6,1},{7,2},{8,3},{9,4},{... | collective-permute-start | bytes 393224 | tf_op jit(solution)/shard_map/ppermute | solution.py:134
  234.7 10.9 %collective-permute-start.11 = (bf16[1,1,32,2048]{3,2,0,1:T(8,128)(2,1)}, bf16[1,1,32,2048]{3,2,0,1:T(8,128)(2,1)S(1)}, u32[]{:S(2)}, u32[]{:S(2)}) collective-permute-start(bf16[1,1,32,2048]{3,2,0,1:T(8,128)(2,1)} %get-tuple-element.34), channel_id=1, source_target_pairs={{0,12},{1,13},{2,14},{3,15},{4,0},{5,1},{6,2},{7,3},{8,4},{9,5},{1... | collective-permute-start | bytes 393224 | tf_op jit(solution)/shard_map/ppermute | solution.py:134
  239.0 7.2 %collective-permute-start.12 = (bf16[1,1,32,2048]{3,2,0,1:T(8,128)(2,1)S(1)}, bf16[1,1,32,2048]{3,2,0,1:T(8,128)(2,1)S(1)}, u32[]{:S(2)}, u32[]{:S(2)}) collective-permute-start(bf16[1,1,32,2048]{3,2,0,1:T(8,128)(2,1)S(1)} %get-tuple-element.33), channel_id=1, source_target_pairs={{0,13},{1,14},{2,15},{3,0},{4,1},{5,2},{6,3},{7,4},{8,5},{9,6},{10... | collective-permute-start | bytes 393224 | tf_op jit(solution)/shard_map/ppermute | solution.py:134
  239.7 10.1 %collective-permute-start.13 = (bf16[1,1,32,2048]{3,2,0,1:T(8,128)(2,1)S(1)}, bf16[1,1,32,2048]{3,2,0,1:T(8,128)(2,1)S(1)}, u32[]{:S(2)}, u32[]{:S(2)}) collective-permute-start(bf16[1,1,32,2048]{3,2,0,1:T(8,128)(2,1)S(1)} %get-tuple-element.32), channel_id=1, source_target_pairs={{0,14},{1,15},{2,0},{3,1},{4,2},{5,3},{6,4},{7,5},{8,6},{9,7},{10,... | collective-permute-start | bytes 393224 | tf_op jit(solution)/shard_map/ppermute | solution.py:134
  242.7 7.8 %collective-permute-start.14 = (bf16[1,1,32,2048]{3,2,0,1:T(8,128)(2,1)S(1)}, bf16[1,1,32,2048]{3,2,0,1:T(8,128)(2,1)S(1)}, u32[]{:S(2)}, u32[]{:S(2)}) collective-permute-start(bf16[1,1,32,2048]{3,2,0,1:T(8,128)(2,1)S(1)} %get-tuple-element.31), channel_id=1, source_target_pairs={{0,15},{1,0},{2,1},{3,2},{4,3},{5,4},{6,5},{7,6},{8,7},{9,8},{10,9... | collective-permute-start | bytes 393224 | tf_op jit(solution)/shard_map/ppermute | solution.py:134
Sparse Core Ops, SparseCore 0:
  9.6 81.6 all-gather.1
  95.1 21.3 reduce-scatter.1
